TPU v7x, 256 devices: a whole 4x4x8 slice. The times are simulated.
256 devices in a mesh: tm: 16 (over x_hi, z), row: 8 (over y, core), col: 2 (over x_lo).
Axes of the slice: x: 4 (x_hi: 2, x_lo: 2; x = x_hi * 2 + x_lo), y: 4, z: 8, core: 2. Of those that a mesh axis runs over, the one named last changes fastest.
Arguments:
- frames: float32 [16, 2048, 1024], P('tm', 'row', 'col'), may hold values from 0 to 200, as said below
- following: float32 [2048, 1024], P('row', 'col'), may hold values from 0 to 200, as said below
Outputs:
- planes: float32 [16, 64, 64, 2048], P('tm', 'row', None, 'col')
Inputs may be any that keep to these rules, and one draw needn't show every extreme that they name: `frames`: detector intensities, never negative. `following`: detector intensities, never negative.
All inputs are finite; a program needn't handle non-finite values.
Results may differ from a plain program's by a relative error of at most 0.000071.
Values sent between devices are 32-bit elements; how exact they have to be, the bound alone decides.
No kernel may reach another device: no remote copies, remote signals or barrier semaphores. Data moves between devices by JAX's collectives and lax.ppermute only.
A program may use at most 128 MiB of HBM per device.

v0:
```python
import jax
import jax.numpy as jnp
import ml_dtypes
import numpy as np
from jax import lax
from jax.experimental import pallas as pl
from jax.experimental.pallas import tpu as pltpu
from jax.sharding import PartitionSpec as P

W = 64
STRIDE = 32
HALF = W // 2
LANES = 128
EPS = 1e-05
F32 = jnp.float32
BF16 = jnp.bfloat16


def parts_of(table, count):
    rest = np.asarray(table, np.float64)
    out = []
    for _ in range(count):
        part = rest.astype(ml_dtypes.bfloat16)
        out.append(part)
        rest = rest - part.astype(np.float64)
    return out


def two_windows(block):
    zero = np.zeros_like(block)
    return np.block([[block, zero], [zero, block]])


def make_tables():
    index = np.arange(W)
    turns = 2.0 * np.pi / W * (index[:, None] * index[None, :] % W)
    cosine, sine = np.cos(turns), np.sin(turns)
    slots = np.arange(HALF)
    down = np.concatenate([cosine[:HALF], -sine[:HALF]], axis=0)
    down[0] = 0.0
    down[HALF] = cosine[HALF]
    hi, lo = parts_of(down, 2)
    down_table = np.concatenate([hi, hi, lo], axis=1)
    across = np.concatenate([two_windows(cosine), two_windows(sine)], axis=1)
    hi, lo, low = parts_of(across, 3)
    across_table = np.concatenate([hi, hi, lo], axis=0)
    fine_table = np.concatenate([hi, hi, hi, lo, lo, low], axis=0)
    up = np.concatenate([2.0 * cosine[:, :HALF], -2.0 * sine[:, :HALF]], axis=1)
    up[:, 0] = 1.0
    up[:, HALF] = cosine[HALF]
    hi, lo = parts_of(up, 2)
    up_table = np.concatenate([hi, hi, lo], axis=1)
    ones = two_windows(np.ones((W, W))).astype(ml_dtypes.bfloat16)
    sum_table = np.concatenate([ones, ones, ones], axis=0)
    return down_table, across_table, fine_table, up_table, sum_table


def mxu(a, b):
    return jnp.dot(a, b, preferred_element_type=F32)


def split2(x):
    hi = x.astype(BF16)
    lo = (x - hi.astype(F32)).astype(BF16)
    return hi, lo


def split3(x):
    hi = x.astype(BF16)
    rest = x - hi.astype(F32)
    mid = rest.astype(BF16)
    low = (rest - mid.astype(F32)).astype(BF16)
    return hi, mid, low


def left32(x):
    return pltpu.roll(x, x.shape[1] - STRIDE, 1)


def eight_tiles(x, shifted):
    count = x.shape[1] // LANES - 1
    return [x[:, LANES * t : LANES * (t + 1)] for t in range(count)] + [
        shifted[:, LANES * t : LANES * (t + 1)] for t in range(count)
    ]


def window_rows(tile_ref, row_ref, col_ref, i, down_count):
    top = STRIDE * i
    lanes = tile_ref.shape[1]
    if i < down_count - 1:
        left = tile_ref[top : top + W, :]
    else:
        left = jnp.concatenate([tile_ref[top : top + STRIDE, :], row_ref[...]], axis=0)
    return jnp.concatenate([left, col_ref[top : top + W, :]], axis=1)


def forward(tile_ref, row_ref, col_ref, down_ref, across_ref, x_ref, stat_ref):
    down_count = x_ref.shape[0]
    tiles = x_ref.shape[1]
    for i in range(down_count):
        pixels = window_rows(tile_ref, row_ref, col_ref, i, down_count)
        base = pixels[0:1, :]
        above = pixels - base
        total = jnp.sum(above, axis=0, keepdims=True)
        centred = above - total * (1.0 / W)
        stat_ref[0, i : i + 1, :] = base
        stat_ref[1, i : i + 1, :] = total
        stat_ref[2, i : i + 1, :] = jnp.sum(centred * centred, axis=0, keepdims=True)
        hi, lo = split2(centred)
        columns = mxu(down_ref[...], jnp.concatenate([hi, lo, hi], axis=0))
        rows = []
        for tile in eight_tiles(columns, left32(columns)):
            hi, lo = split2(tile)
            rows.append(jnp.concatenate([hi, lo, hi], axis=1))
        spectrum = mxu(jnp.concatenate(rows, axis=0), across_ref[...])
        for k in range(tiles):
            block = spectrum[W * k : W * (k + 1)]
            x_ref[i, k, 0:HALF, :] = block[:HALF, :LANES] + block[HALF:, LANES:]
            x_ref[i, k, HALF:W, :] = block[HALF:, :LANES] - block[:HALF, LANES:]


def stacked(x):
    return jnp.concatenate(eight_tiles(x, left32(x)), axis=0)


def statistics(stat_ref, sum_ref, fine_ref):
    base = stacked(stat_ref[0])
    total = stacked(stat_ref[1])
    squares = stacked(stat_ref[2])
    mean_base = mxu(jnp.concatenate(split3(base), axis=1), sum_ref[...]) * (1.0 / W)
    level = total + float(W) * (base - mean_base)
    energy = squares + level * level * (1.0 / W)
    both = jnp.concatenate([level, energy], axis=0)
    sums = mxu(jnp.concatenate(split3(both), axis=1), sum_ref[...])
    count = level.shape[0]
    mean_level = sums[:count] * (1.0 / W)
    variance = (sums[count:] - mean_level * mean_level) * (1.0 / (W * W))
    scale = lax.rsqrt(jnp.maximum(variance, 0.0) + EPS)
    hi, mid, low = split3(level - mean_level)
    wave = mxu(jnp.concatenate([hi, mid, low, hi, mid, hi], axis=1), fine_ref[...])
    lane = lax.broadcasted_iota(jnp.int32, (count, LANES), 1)
    inside = lax.rem(lane, W) != 0
    real = jnp.where(inside, wave[:, :LANES], 0.0)
    imaginary = jnp.where(inside, -wave[:, LANES:], 0.0)
    return real, imaginary, scale


def frequency32(x_ref):
    down_count, tiles = x_ref.shape[0], x_ref.shape[1]
    minus = jnp.concatenate([x_ref[i, k, 0:1, :] for k in range(tiles) for i in range(down_count)], axis=0)
    real = jnp.concatenate([x_ref[i, k, HALF : HALF + 1, :] for k in range(tiles) for i in range(down_count)], axis=0)
    return real, -minus


def cross(a_real, a_imaginary, b_real, b_imaginary):
    return (
        a_real * b_real + a_imaginary * b_imaginary,
        a_real * b_imaginary - a_imaginary * b_real,
    )


def across_back(blocks, across_ref):
    rows = []
    for block in blocks:
        hi, lo = split2(block)
        rows.append(jnp.concatenate([hi, lo, hi], axis=1))
    return mxu(jnp.concatenate(rows, axis=0), across_ref[...])


def edge_rows(first_ref, second_ref, first_stat, second_stat, tables, edge_ref, scale_ref):
    down_ref, across_ref, fine_ref, up_ref, sum_ref = tables
    a_real, a_imaginary, a_scale = statistics(first_stat, sum_ref, fine_ref)
    b_real, b_imaginary, b_scale = statistics(second_stat, sum_ref, fine_ref)
    scale = a_scale * b_scale * (1.0 / (W * W * W))
    scale_ref[...] = scale
    p_real, p_imaginary = cross(a_real, a_imaginary, b_real, b_imaginary)
    r_real, r_imaginary = cross(*frequency32(first_ref), *frequency32(second_ref))
    back = across_back([p_real, p_imaginary, r_real, r_imaginary], across_ref)
    n = scale.shape[0]
    edge_ref[0] = (back[:n, :LANES] - back[n : 2 * n, LANES:]) * scale
    edge_ref[1] = (back[2 * n : 3 * n, :LANES] - back[3 * n :, LANES:]) * scale


def backward(first_ref, second_ref, across_ref, up_ref, edge_ref, scale_ref, out_ref):
    down_count, tiles = first_ref.shape[0], first_ref.shape[1]
    lane = lax.broadcasted_iota(jnp.int32, (W, LANES), 1)
    sublane = lax.broadcasted_iota(jnp.int32, (HALF, LANES), 0)
    left = lane < W
    for i in range(down_count):
        blocks = []
        for k in range(tiles):
            blocks.append(
                jnp.concatenate(
                    cross(
                        first_ref[i, k, 0:HALF, :],
                        first_ref[i, k, HALF:W, :],
                        second_ref[i, k, 0:HALF, :],
                        second_ref[i, k, HALF:W, :],
                    ),
                    axis=0,
                )
            )
        back = across_back(blocks, across_ref)
        lines = []
        for k in range(tiles):
            block = back[W * k : W * (k + 1)]
            at = down_count * k + i
            scale = scale_ref[at : at + 1, :]
            real = (block[:HALF, :LANES] - block[HALF:, LANES:]) * scale
            imaginary = (block[HALF:, :LANES] + block[:HALF, LANES:]) * scale
            real = jnp.where(sublane == 0, edge_ref[0, at : at + 1, :], real)
            imaginary = jnp.where(sublane == 0, edge_ref[1, at : at + 1, :], imaginary)
            lines.append(jnp.concatenate([real, imaginary], axis=0))
        pairs = []
        for t in range(tiles // 2):
            even, odd = lines[t], lines[tiles // 2 + t]
            pairs.append(jnp.where(left, even, pltpu.roll(odd, W, 1)))
            pairs.append(jnp.where(left, pltpu.roll(even, W, 1), odd))
        hi, lo = split2(jnp.concatenate(pairs, axis=1))
        out_ref[0, i] = mxu(up_ref[...], jnp.concatenate([hi, lo, hi], axis=0))


def whole_kernel(
    tile_ref, row_ref, col_ref, next_ref, next_row_ref, next_col_ref,
    down_ref, across_ref, fine_ref, up_ref, sum_ref,
    out_ref,
    first_ref, second_ref, first_stat, second_stat, edge_ref, scale_ref,
):
    tables = (down_ref, across_ref, fine_ref, up_ref, sum_ref)
    forward(tile_ref, row_ref, col_ref, down_ref, across_ref, first_ref, first_stat)
    forward(next_ref, next_row_ref, next_col_ref, down_ref, across_ref, second_ref, second_stat)
    edge_rows(first_ref, second_ref, first_stat, second_stat, tables, edge_ref, scale_ref)
    backward(first_ref, second_ref, across_ref, up_ref, edge_ref, scale_ref, out_ref)


def correlate(tile, row, col, following, next_row, next_col):
    height, breadth = tile.shape
    down_count = height // STRIDE
    tiles = 2 * breadth // LANES
    wide = breadth + LANES
    tables = [jnp.asarray(t, BF16) for t in make_tables()]
    scratch = [
        pltpu.VMEM((down_count, tiles, W, LANES), F32),
        pltpu.VMEM((down_count, tiles, W, LANES), F32),
        pltpu.VMEM((3, down_count, wide), F32),
        pltpu.VMEM((3, down_count, wide), F32),
        pltpu.VMEM((2, tiles * down_count, LANES), F32),
        pltpu.VMEM((tiles * down_count, LANES), F32),
    ]
    return pl.pallas_call(
        whole_kernel,
        out_shape=jax.ShapeDtypeStruct((1, down_count, W, 2 * breadth), F32),
        in_specs=[pl.BlockSpec(memory_space=pltpu.VMEM)] * 11,
        out_specs=pl.BlockSpec(memory_space=pltpu.VMEM),
        scratch_shapes=scratch,
        compiler_params=pltpu.CompilerParams(vmem_limit_bytes=40 << 20),
        name="correlate",
    )(tile, row, col, following, next_row, next_col, *tables)


def shifted(x, axis, by):
    devices = lax.axis_size(axis)
    pairs = [(i, i + by) for i in range(devices) if 0 <= i + by < devices]
    return lax.ppermute(x, axis, pairs)


def on_device(frames, following):
    at_end = lax.axis_index("tm") == lax.axis_size("tm") - 1
    tile = frames[0]
    arriving = shifted(tile, "tm", -1)
    both = jnp.stack([tile[:STRIDE], following[:STRIDE]])
    below = shifted(both, "row", -1)
    slab = jnp.concatenate([jnp.stack([tile, following])[:, :, :LANES], below[:, :, :LANES]], axis=1)
    beside = shifted(slab, "col", -1)
    next_row = jnp.where(at_end, below[1], shifted(below[0], "tm", -1))
    next_col = jnp.where(at_end, beside[1], shifted(beside[0], "tm", -1))
    upcoming = jnp.where(at_end, following, arriving)
    return correlate(tile, below[0], beside[0], upcoming, next_row, next_col)


def solution(mesh):
    in_specs = (P("tm", "row", "col"), P("row", "col"))
    out_specs = P("tm", "row", None, "col")
    return jax.shard_map(
        on_device, mesh=mesh, in_specs=in_specs, out_specs=out_specs, check_vma=False
    )
```

profile of v0, /device:TPU:23, one launch (start us, length us, event | category | flops | bytes accessed | tf_op | source)
XLA Modules:
  0.0 48.5 jit_solution(4812381239370330379)
XLA Ops:
  0.0 0.0 copy-start
  0.0 0.0 copy-start.6
  0.0 0.9 %slice.27 = f32[1,32,512]{2,1,0:T(8,128)S(1)} slice(f32[1,256,512]{2,1,0:T(8,128)} %param.7), slice={[0:1], [0:32], [0:512]} | slice | bytes 131072 | tf_op jit(solution)/shard_map/slice | solution.py:271
  0.9 0.8 %slice_bitcast_fusion.4 = f32[1,32,512]{2,1,0:T(8,128)S(1)} fusion(f32[256,512]{1,0:T(8,128)} %param.8), kind=kLoop, calls=%fused_computation.10 | loop fusion | bytes 131072 | tf_op jit(solution)/shard_map/stack | solution.py:271
  1.8 0.0 copy-start.1
  1.8 0.0 copy-start.2
  1.8 0.0 copy-start.3
  1.8 0.0 copy-start.4
  1.8 0.0 copy-start.5
  1.9 2.7 %collective-permute-start = (f32[2,32,512]{2,1,0:T(8,128)S(1)}, f32[2,32,512]{2,1,0:T(8,128)S(1)}, u32[]{:S(2)}, u32[]{:S(2)}) collective-permute-start(f32[2,32,512]{2,1,0:T(8,128)S(1)} %pad_maximum_fusion.1), channel_id=1, source_target_pairs={{2,0},{4,2},{6,4},{8,6},{10,8},{12,10},{14,12},{3,1},{5,3},{7,5},{... | collective-permute-start | bytes 393224 | tf_op jit(solution)/shard_map/ppermute | solution.py:264
  4.6 3.7 %collective-permute-done = f32[2,32,512]{2,1,0:T(8,128)S(1)} collective-permute-done((f32[2,32,512]{2,1,0:T(8,128)S(1)}, f32[2,32,512]{2,1,0:T(8,128)S(1)}, u32[]{:S(2)}, u32[]{:S(2)}) %collective-permute-start) | collective-permute-done | bytes 131104 | tf_op jit(solution)/shard_map/ppermute | solution.py:264
  8.3 1.0 %fusion = f32[2,288,128]{2,1,0:T(8,128)S(1)} fusion(f32[1,256,512]{2,1,0:T(8,128)} %bitcast.18, f32[1,256,512]{2,1,0:T(8,128)} %param.7, f32[2,32,128]{2,1,0:T(8,128)S(1)} %slice.36), kind=kLoop, calls=%fused_computation.1 | loop fusion | flops 147456 | bytes 1376256 | tf_op jit(solution)/shard_map/concatenate | solution.py:273
  9.3 2.5 %collective-permute-start.1 = (f32[2,288,128]{2,1,0:T(8,128)S(1)}, f32[2,288,128]{2,1,0:T(8,128)S(1)}, u32[]{:S(2)}, u32[]{:S(2)}) collective-permute-start(f32[2,288,128]{2,1,0:T(8,128)S(1)} %fusion), channel_id=1, source_target_pairs={{1,0},{3,2},{5,4},{7,6},{9,8},{11,10},{13,12},{15,14},{17,16},{19,... | collective-permute-start | bytes 884744 | tf_op jit(solution)/shard_map/ppermute | solution.py:264
  11.8 8.0 %collective-permute-start.3 = (f32[32,512]{1,0:T(8,128)S(1)}, f32[32,512]{1,0:T(8,128)S(1)}, u32[]{:S(2)}, u32[]{:S(2)}) collective-permute-start(f32[32,512]{1,0:T(8,128)S(1)} %slice_bitcast_fusion.3.row_ref), channel_id=1, source_target_pairs={{16,0},{32,16},{48,32},{64,48},{80,64},{96,80},{112,96},{128,112},... | collective-permute-start | bytes 196616 | tf_op jit(solution)/shard_map/ppermute | solution.py:264
  19.8 0.0 copy-done
  19.8 2.6 %collective-permute-start.2 = (f32[256,512]{1,0:T(8,128)S(1)}, f32[256,512]{1,0:T(8,128)S(1)}, u32[]{:S(2)}, u32[]{:S(2)}) collective-permute-start(f32[256,512]{1,0:T(8,128)S(1)} %bitcast.16), channel_id=1, source_target_pairs={{16,0},{32,16},{48,32},{64,48},{80,64},{96,80},{112,96},{128,112},... | collective-permute-start | bytes 1572872 | tf_op jit(solution)/shard_map/ppermute | solution.py:264
  22.5 0.0 collective-permute-done.3
  22.5 0.0 collective-permute-done.1
  22.5 6.3 %collective-permute-start.4 = (f32[288,128]{1,0:T(8,128)S(1)}, f32[288,128]{1,0:T(8,128)S(1)}, u32[]{:S(2)}, u32[]{:S(2)}) collective-permute-start(f32[288,128]{1,0:T(8,128)S(1)} %slice_bitcast_fusion.1.col_ref), channel_id=1, source_target_pairs={{16,0},{32,16},{48,32},{64,48},{80,64},{96,80},{112,96},{128,112},... | collective-permute-start | bytes 442376 | tf_op jit(solution)/shard_map/ppermute | solution.py:264
  28.8 6.8 %collective-permute-done.2 = f32[256,512]{1,0:T(8,128)S(1)} collective-permute-done((f32[256,512]{1,0:T(8,128)S(1)}, f32[256,512]{1,0:T(8,128)S(1)}, u32[]{:S(2)}, u32[]{:S(2)}) %collective-permute-start.2) | collective-permute-done | bytes 524320 | tf_op jit(solution)/shard_map/ppermute | solution.py:264
  35.7 0.0 copy-done.6
  35.7 0.1 broadcast_select_fusion.next_ref
  35.7 2.7 %collective-permute-done.4 = f32[288,128]{1,0:T(8,128)S(1)} collective-permute-done((f32[288,128]{1,0:T(8,128)S(1)}, f32[288,128]{1,0:T(8,128)S(1)}, u32[]{:S(2)}, u32[]{:S(2)}) %collective-permute-start.4) | collective-permute-done | bytes 147488 | tf_op jit(solution)/shard_map/ppermute | solution.py:264
  38.5 0.0 copy-done.1
  38.5 0.0 copy-done.2
  38.5 0.0 copy-done.3
  38.5 0.0 copy-done.4
  38.5 0.0 copy-done.5
  38.6 9.9 %correlate.1 = f32[1,8,64,1024]{3,2,1,0:T(8,128)} custom-call(f32[256,512]{1,0:T(8,128)S(1)} %bitcast.17, f32[32,512]{1,0:T(8,128)S(1)} %slice_bitcast_fusion.3.row_ref, f32[288,128]{1,0:T(8,128)S(1)} %slice_bitcast_fusion.1.col_ref, f32[256,512]{1,0:T(8,128)S(1)} %broadcast_select_fusion.next_ref, f32[32,512]{1,0:T(8,128)S(1)} %fusion.2.next_row_ref, ...), custom_call_target="tpu_custom_call" | custom-call | tf_op jit(solution)/shard_map/correlate/pallas_call | solution.py:250
  (6 shorter events, 0.1 us)
Async XLA Ops:
  0.0 19.8 %copy-start = (f32[1,256,512]{2,1,0:T(8,128)S(1)}, f32[1,256,512]{2,1,0:T(8,128)}, u32[]{:S(2)}) copy-start(f32[1,256,512]{2,1,0:T(8,128)} %param.7) | copy-start | bytes 1572868
  0.0 35.7 %copy-start.6 = (f32[256,512]{1,0:T(8,128)S(1)}, f32[256,512]{1,0:T(8,128)}, u32[]{:S(2)}) copy-start(f32[256,512]{1,0:T(8,128)} %param.8) | copy-start | bytes 1572868
  1.8 36.7 %copy-start.1 = (bf16[768,256]{1,0:T(8,128)(2,1)S(1)}, bf16[768,256]{1,0:T(8,128)(2,1)}, u32[]{:S(2)}) copy-start(bf16[768,256]{1,0:T(8,128)(2,1)} %constant.19.clone.fine_ref) | copy-start | bytes 1179652
  1.8 36.7 %copy-start.2 = (bf16[384,256]{1,0:T(8,128)(2,1)S(1)}, bf16[384,256]{1,0:T(8,128)(2,1)}, u32[]{:S(2)}) copy-start(bf16[384,256]{1,0:T(8,128)(2,1)} %constant.18.clone.across_ref) | copy-start | bytes 589828
  1.8 36.7 %copy-start.3 = (bf16[384,128]{1,0:T(8,128)(2,1)S(1)}, bf16[384,128]{1,0:T(8,128)(2,1)}, u32[]{:S(2)}) copy-start(bf16[384,128]{1,0:T(8,128)(2,1)} %constant.21.clone.sum_ref) | copy-start | bytes 294916
  1.8 36.7 %copy-start.4 = (bf16[64,192]{1,0:T(8,128)(2,1)S(1)}, bf16[64,192]{1,0:T(8,128)(2,1)}, u32[]{:S(2)}) copy-start(bf16[64,192]{1,0:T(8,128)(2,1)} %constant.20.clone.up_ref) | copy-start | bytes 73732
  1.8 36.7 %copy-start.5 = (bf16[64,192]{1,0:T(8,128)(2,1)S(1)}, bf16[64,192]{1,0:T(8,128)(2,1)}, u32[]{:S(2)}) copy-start(bf16[64,192]{1,0:T(8,128)(2,1)} %constant.17.clone.down_ref) | copy-start | bytes 73732
  1.9 6.4 %collective-permute-start = (f32[2,32,512]{2,1,0:T(8,128)S(1)}, f32[2,32,512]{2,1,0:T(8,128)S(1)}, u32[]{:S(2)}, u32[]{:S(2)}) collective-permute-start(f32[2,32,512]{2,1,0:T(8,128)S(1)} %pad_maximum_fusion.1), channel_id=1, source_target_pairs={{2,0},{4,2},{6,4},{8,6},{10,8},{12,10},{14,12},{3,1},{5,3},{7,5},{... | collective-permute-start | bytes 393224 | tf_op jit(solution)/shard_map/ppermute | solution.py:264
  9.3 13.2 %collective-permute-start.1 = (f32[2,288,128]{2,1,0:T(8,128)S(1)}, f32[2,288,128]{2,1,0:T(8,128)S(1)}, u32[]{:S(2)}, u32[]{:S(2)}) collective-permute-start(f32[2,288,128]{2,1,0:T(8,128)S(1)} %fusion), channel_id=1, source_target_pairs={{1,0},{3,2},{5,4},{7,6},{9,8},{11,10},{13,12},{15,14},{17,16},{19,... | collective-permute-start | bytes 884744 | tf_op jit(solution)/shard_map/ppermute | solution.py:264
  11.8 10.7 %collective-permute-start.3 = (f32[32,512]{1,0:T(8,128)S(1)}, f32[32,512]{1,0:T(8,128)S(1)}, u32[]{:S(2)}, u32[]{:S(2)}) collective-permute-start(f32[32,512]{1,0:T(8,128)S(1)} %slice_bitcast_fusion.3.row_ref), channel_id=1, source_target_pairs={{16,0},{32,16},{48,32},{64,48},{80,64},{96,80},{112,96},{128,112},... | collective-permute-start | bytes 196616 | tf_op jit(solution)/shard_map/ppermute | solution.py:264
  19.8 15.8 %collective-permute-start.2 = (f32[256,512]{1,0:T(8,128)S(1)}, f32[256,512]{1,0:T(8,128)S(1)}, u32[]{:S(2)}, u32[]{:S(2)}) collective-permute-start(f32[256,512]{1,0:T(8,128)S(1)} %bitcast.16), channel_id=1, source_target_pairs={{16,0},{32,16},{48,32},{64,48},{80,64},{96,80},{112,96},{128,112},... | collective-permute-start | bytes 1572872 | tf_op jit(solution)/shard_map/ppermute | solution.py:264
  22.5 16.0 %collective-permute-start.4 = (f32[288,128]{1,0:T(8,128)S(1)}, f32[288,128]{1,0:T(8,128)S(1)}, u32[]{:S(2)}, u32[]{:S(2)}) collective-permute-start(f32[288,128]{1,0:T(8,128)S(1)} %slice_bitcast_fusion.1.col_ref), channel_id=1, source_target_pairs={{16,0},{32,16},{48,32},{64,48},{80,64},{96,80},{112,96},{128,112},... | collective-permute-start | bytes 442376 | tf_op jit(solution)/shard_map/ppermute | solution.py:264
where the time goes:
time: 48.7 us; the launch traced here: 48.5 us
  starting transfers between devices  22.2 us (46%)
  waiting for transfers between devices  13.3 us (27%)
  Pallas kernels  9.89 us (20%)
  local copies, waits for them, and re-layouts  1.84 us (4%)
  other arithmetic  1.11 us (2%)
    ppermute x5, starting transfers between devices, shifted(): return lax.ppermute(x, axis, pairs)  22.2 us
    ppermute x5, waiting for transfers between devices, shifted(): return lax.ppermute(x, axis, pairs)  13.3 us
    pallas_call x1, Pallas kernels, correlate(): pl.pallas_call(whole_kernel, out_shape=jax.ShapeDtypeStruct((1, down_coun...  9.89 us
    concatenate x1, other arithmetic, on_device(): jnp.concatenate([jnp.stack([tile, following])[:, :, :LANES], below[:, :,...  0.99 us
  transfers between devices with their start and end apart: 5, of which 3 were waited for; matrix products, arithmetic and copies ran while one was open for 0% of the time, Pallas kernels for 0%

commit v1 on v0

--- a/solution.py
+++ b/solution.py
@@ -1,3 +1,5 @@
+import functools
+
 import jax
 import jax.numpy as jnp
 import ml_dtypes
@@ -7,6 +9,7 @@
 from jax.experimental.pallas import tpu as pltpu
 from jax.sharding import PartitionSpec as P
 
+
 W = 64
 STRIDE = 32
 HALF = W // 2
@@ -14,6 +17,8 @@
 EPS = 1e-05
 F32 = jnp.float32
 BF16 = jnp.bfloat16
+FIRST_VMEM = 8 << 20
+SECOND_VMEM = 16 << 20
 
 
 def parts_of(table, count):
@@ -35,7 +40,6 @@
     index = np.arange(W)
     turns = 2.0 * np.pi / W * (index[:, None] * index[None, :] % W)
     cosine, sine = np.cos(turns), np.sin(turns)
-    slots = np.arange(HALF)
     down = np.concatenate([cosine[:HALF], -sine[:HALF]], axis=0)
     down[0] = 0.0
     down[HALF] = cosine[HALF]
@@ -84,21 +88,33 @@
     ]
 
 
-def window_rows(tile_ref, row_ref, col_ref, i, down_count):
+def column_block(pack, corner, b):
+    blocks = 2 * LANES // STRIDE
+    if b < blocks:
+        return turned(pack[STRIDE * (b % 2) : STRIDE * (b % 2) + STRIDE, :], b // 2)
+    return jnp.concatenate([turned(corner, q) for q in range(LANES // STRIDE)], axis=0)
+
+
+def turned(x, quarter):
+    return pltpu.roll(x, LANES - STRIDE * quarter, 1) if quarter else x
+
+
+def window_rows(tile, rims, i, down_count):
+    row, pack, corner = rims
     top = STRIDE * i
-    lanes = tile_ref.shape[1]
     if i < down_count - 1:
-        left = tile_ref[top : top + W, :]
+        left = tile[top : top + W, :]
     else:
-        left = jnp.concatenate([tile_ref[top : top + STRIDE, :], row_ref[...]], axis=0)
-    return jnp.concatenate([left, col_ref[top : top + W, :]], axis=1)
-
-
-def forward(tile_ref, row_ref, col_ref, down_ref, across_ref, x_ref, stat_ref):
+        left = jnp.concatenate([tile[top : top + STRIDE, :], row], axis=0)
+    right = jnp.concatenate([column_block(pack, corner, i), column_block(pack, corner, i + 1)], axis=0)
+    return jnp.concatenate([left, right], axis=1)
+
+
+def forward(tile, rims, down_ref, across_ref, x_ref, stat_ref):
     down_count = x_ref.shape[0]
     tiles = x_ref.shape[1]
     for i in range(down_count):
-        pixels = window_rows(tile_ref, row_ref, col_ref, i, down_count)
+        pixels = window_rows(tile, rims, i, down_count)
         base = pixels[0:1, :]
         above = pixels - base
         total = jnp.sum(above, axis=0, keepdims=True)
@@ -109,8 +125,8 @@
         hi, lo = split2(centred)
         columns = mxu(down_ref[...], jnp.concatenate([hi, lo, hi], axis=0))
         rows = []
-        for tile in eight_tiles(columns, left32(columns)):
-            hi, lo = split2(tile)
+        for piece in eight_tiles(columns, left32(columns)):
+            hi, lo = split2(piece)
             rows.append(jnp.concatenate([hi, lo, hi], axis=1))
         spectrum = mxu(jnp.concatenate(rows, axis=0), across_ref[...])
         for k in range(tiles):
@@ -168,7 +184,7 @@
 
 
 def edge_rows(first_ref, second_ref, first_stat, second_stat, tables, edge_ref, scale_ref):
-    down_ref, across_ref, fine_ref, up_ref, sum_ref = tables
+    _, across_ref, fine_ref, _, sum_ref = tables
     a_real, a_imaginary, a_scale = statistics(first_stat, sum_ref, fine_ref)
     b_real, b_imaginary, b_scale = statistics(second_stat, sum_ref, fine_ref)
     scale = a_scale * b_scale * (1.0 / (W * W * W))
@@ -181,7 +197,7 @@
     edge_ref[1] = (back[2 * n : 3 * n, :LANES] - back[3 * n :, LANES:]) * scale
 
 
-def backward(first_ref, second_ref, across_ref, up_ref, edge_ref, scale_ref, out_ref):
+def backward(first_ref, second_ref, across_ref, up_ref, edge_ref, scale_ref, out_ref, finished):
     down_count, tiles = first_ref.shape[0], first_ref.shape[1]
     lane = lax.broadcasted_iota(jnp.int32, (W, LANES), 1)
     sublane = lax.broadcasted_iota(jnp.int32, (HALF, LANES), 0)
@@ -217,45 +233,139 @@
             pairs.append(jnp.where(left, even, pltpu.roll(odd, W, 1)))
             pairs.append(jnp.where(left, pltpu.roll(even, W, 1), odd))
         hi, lo = split2(jnp.concatenate(pairs, axis=1))
-        out_ref[0, i] = mxu(up_ref[...], jnp.concatenate([hi, lo, hi], axis=0))
-
-
-def whole_kernel(
-    tile_ref, row_ref, col_ref, next_ref, next_row_ref, next_col_ref,
+        out_ref[i] = mxu(up_ref[...], jnp.concatenate([hi, lo, hi], axis=0))
+        finished(i)
+
+
+def packed_columns(x):
+    rows = x.shape[0] // 4
+    lane = lax.broadcasted_iota(jnp.int32, (rows, LANES), 1)
+    out = x[:rows]
+    for q in range(1, 4):
+        out = jnp.where(lane < STRIDE * q, out, pltpu.roll(x[rows * q : rows * (q + 1)], STRIDE * q, 1))
+    return out
+
+
+def strips_kernel(row_ref, col_ref, next_row_ref, next_col_ref, out_row_ref, out_col_ref, out_corner_ref):
+    for n, (row, col) in enumerate(((row_ref, col_ref), (next_row_ref, next_col_ref))):
+        out_row_ref[n] = row[...].reshape(row.shape[-2:])
+        slab = col[...].reshape(col.shape[-2:])
+        out_col_ref[n] = packed_columns(slab)
+        out_corner_ref[n] = packed_columns(slab[:STRIDE])
+
+
+def strips(frames, following):
+    height, breadth = following.shape
+    return pl.pallas_call(
+        strips_kernel,
+        grid=(1,),
+        out_shape=(
+            jax.ShapeDtypeStruct((2, STRIDE, breadth), F32),
+            jax.ShapeDtypeStruct((2, height // 4, LANES), F32),
+            jax.ShapeDtypeStruct((2, STRIDE // 4, LANES), F32),
+        ),
+        in_specs=[
+            pl.BlockSpec((1, STRIDE, breadth), lambda g: (0, 0, 0)),
+            pl.BlockSpec((1, height, LANES), lambda g: (0, 0, 0)),
+            pl.BlockSpec((STRIDE, breadth), lambda g: (0, 0)),
+            pl.BlockSpec((height, LANES), lambda g: (0, 0)),
+        ],
+        out_specs=(
+            pl.BlockSpec((2, STRIDE, breadth), lambda g: (0, 0, 0)),
+            pl.BlockSpec((2, height // 4, LANES), lambda g: (0, 0, 0)),
+            pl.BlockSpec((2, STRIDE // 4, LANES), lambda g: (0, 0, 0)),
+        ),
+        name="strips",
+    )(frames, frames, following, following)
+
+
+def first_kernel(lasts, tile_ref, row_ref, col_ref, corner_ref, down_ref, across_ref, x_ref, stat_ref, send_ref, next_ref):
+    row_last, col_last = lasts()
+    for n, out in enumerate((send_ref, next_ref)):
+        row = jnp.where(row_last, 0.0, row_ref[n])
+        pack = jnp.where(col_last, 0.0, col_ref[n])
+        corner = jnp.where(jnp.logical_or(row_last, col_last), 0.0, corner_ref[n])
+        pieces = [row[:, LANES * t : LANES * (t + 1)] for t in range(row.shape[1] // LANES)]
+        out[...] = jnp.concatenate(pieces + [pack, corner], axis=0)
+        if n == 0:
+            rims = (row, pack, corner)
+    forward(tile_ref[...], rims, down_ref, across_ref, x_ref, stat_ref)
+
+
+def second_kernel(
+    at_end, tile_ref, following_ref, rim_ref, following_rim_ref, first_ref, first_stat,
     down_ref, across_ref, fine_ref, up_ref, sum_ref,
     out_ref,
-    first_ref, second_ref, first_stat, second_stat, edge_ref, scale_ref,
+    second_ref, second_stat, edge_ref, scale_ref, plane_ref, sems,
 ):
+    last = at_end()
+    tile = jnp.where(last, following_ref[...], tile_ref[...])
+    rim = jnp.where(last, following_rim_ref[...], rim_ref[...])
     tables = (down_ref, across_ref, fine_ref, up_ref, sum_ref)
-    forward(tile_ref, row_ref, col_ref, down_ref, across_ref, first_ref, first_stat)
-    forward(next_ref, next_row_ref, next_col_ref, down_ref, across_ref, second_ref, second_stat)
+    count = tile.shape[1] // LANES
+    row = jnp.concatenate([rim[STRIDE * t : STRIDE * (t + 1)] for t in range(count)], axis=1)
+    at = STRIDE * count
+    rows = tile.shape[0] // 4
+    rims = (row, rim[at : at + rows], rim[at + rows : at + rows + STRIDE // 4])
+    forward(tile, rims, down_ref, across_ref, second_ref, second_stat)
     edge_rows(first_ref, second_ref, first_stat, second_stat, tables, edge_ref, scale_ref)
-    backward(first_ref, second_ref, across_ref, up_ref, edge_ref, scale_ref, out_ref)
-
-
-def correlate(tile, row, col, following, next_row, next_col):
-    height, breadth = tile.shape
+    copies = []
+
+    def finished(i):
+        copies.append(pltpu.make_async_copy(plane_ref.at[i], out_ref.at[0, i], sems.at[i]))
+        copies[-1].start()
+
+    backward(first_ref, second_ref, across_ref, up_ref, edge_ref, scale_ref, plane_ref, finished)
+    for copy in copies:
+        copy.wait()
+
+
+ANY = pl.BlockSpec(memory_space=pl.ANY)
+VMEM = pl.BlockSpec(memory_space=pltpu.VMEM)
+
+
+def sizes(height, breadth):
     down_count = height // STRIDE
     tiles = 2 * breadth // LANES
-    wide = breadth + LANES
-    tables = [jnp.asarray(t, BF16) for t in make_tables()]
-    scratch = [
-        pltpu.VMEM((down_count, tiles, W, LANES), F32),
-        pltpu.VMEM((down_count, tiles, W, LANES), F32),
-        pltpu.VMEM((3, down_count, wide), F32),
-        pltpu.VMEM((3, down_count, wide), F32),
-        pltpu.VMEM((2, tiles * down_count, LANES), F32),
-        pltpu.VMEM((tiles * down_count, LANES), F32),
-    ]
+    spectrum = (down_count, tiles, W, LANES)
+    stat = (3, down_count, breadth + LANES)
+    rim = (STRIDE * (breadth // LANES) + height // 4 + STRIDE // 4, LANES)
+    return down_count, tiles, spectrum, stat, rim
+
+
+def first(tile, row, col, corner, lasts, tables):
+    _, _, spectrum, stat, rim = sizes(*tile.shape)
     return pl.pallas_call(
-        whole_kernel,
+        functools.partial(first_kernel, lasts),
+        out_shape=tuple(jax.ShapeDtypeStruct(shape, F32) for shape in (spectrum, stat, rim, rim)),
+        in_specs=[VMEM] * 6,
+        out_specs=(VMEM,) * 4,
+        compiler_params=pltpu.CompilerParams(vmem_limit_bytes=FIRST_VMEM),
+        cost_estimate=pl.CostEstimate(flops=3 * 10**9, bytes_accessed=3 << 20, transcendentals=0),
+        name="first",
+    )(tile, row, col, corner, *tables[:2])
+
+
+def second(at_end, tile, following, rims, following_rims, spectrum, stat, tables):
+    height, breadth = tile.shape
+    down_count, tiles, shape, stat_shape, _ = sizes(height, breadth)
+    return pl.pallas_call(
+        functools.partial(second_kernel, at_end),
         out_shape=jax.ShapeDtypeStruct((1, down_count, W, 2 * breadth), F32),
-        in_specs=[pl.BlockSpec(memory_space=pltpu.VMEM)] * 11,
-        out_specs=pl.BlockSpec(memory_space=pltpu.VMEM),
-        scratch_shapes=scratch,
-        compiler_params=pltpu.CompilerParams(vmem_limit_bytes=40 << 20),
-        name="correlate",
-    )(tile, row, col, following, next_row, next_col, *tables)
+        in_specs=[VMEM] * 11,
+        out_specs=ANY,
+        scratch_shapes=[
+            pltpu.VMEM(shape, F32),
+            pltpu.VMEM(stat_shape, F32),
+            pltpu.VMEM((2, tiles * down_count, LANES), F32),
+            pltpu.VMEM((tiles * down_count, LANES), F32),
+            pltpu.VMEM((down_count, W, 2 * breadth), F32),
+            pltpu.SemaphoreType.DMA((down_count,)),
+        ],
+        compiler_params=pltpu.CompilerParams(vmem_limit_bytes=SECOND_VMEM),
+        cost_estimate=pl.CostEstimate(flops=8 * 10**9, bytes_accessed=5 << 20, transcendentals=0),
+        name="second",
+    )(tile, following, rims, following_rims, spectrum, stat, *tables)
 
 
 def shifted(x, axis, by):
@@ -264,23 +374,44 @@
     return lax.ppermute(x, axis, pairs)
 
 
+def turned_down(x, *axes):
+    counts = [lax.axis_size(axis) for axis in axes]
+    pairs = []
+    for source in np.ndindex(*counts):
+        target = tuple((s - 1) % n for s, n in zip(source, counts))
+        pairs.append((int(np.ravel_multi_index(source, counts)), int(np.ravel_multi_index(target, counts))))
+    return lax.ppermute(x, axes if len(axes) > 1 else axes[0], pairs)
+
+
+def lasts():
+    return (
+        lax.axis_index("row") == lax.axis_size("row") - 1,
+        lax.axis_index("col") == lax.axis_size("col") - 1,
+    )
+
+
+def at_end():
+    return lax.axis_index("tm") == lax.axis_size("tm") - 1
+
+
 def on_device(frames, following):
-    at_end = lax.axis_index("tm") == lax.axis_size("tm") - 1
+    tables = [jnp.asarray(t, BF16) for t in make_tables()]
     tile = frames[0]
     arriving = shifted(tile, "tm", -1)
-    both = jnp.stack([tile[:STRIDE], following[:STRIDE]])
-    below = shifted(both, "row", -1)
-    slab = jnp.concatenate([jnp.stack([tile, following])[:, :, :LANES], below[:, :, :LANES]], axis=1)
-    beside = shifted(slab, "col", -1)
-    next_row = jnp.where(at_end, below[1], shifted(below[0], "tm", -1))
-    next_col = jnp.where(at_end, beside[1], shifted(beside[0], "tm", -1))
-    upcoming = jnp.where(at_end, following, arriving)
-    return correlate(tile, below[0], beside[0], upcoming, next_row, next_col)
+    rows, cols, corners = strips(frames, following)
+    rows = turned_down(rows, "row")
+    cols = turned_down(cols, "col")
+    corners = turned_down(corners, "row", "col")
+    spectrum, stat, send, following_rims = first(tile, rows, cols, corners, lasts, tables)
+    rims = shifted(send, "tm", -1)
+    return second(at_end, arriving, following, rims, following_rims, spectrum, stat, tables)
 
 
 def solution(mesh):
     in_specs = (P("tm", "row", "col"), P("row", "col"))
     out_specs = P("tm", "row", None, "col")
+
+
     return jax.shard_map(
         on_device, mesh=mesh, in_specs=in_specs, out_specs=out_specs, check_vma=False
     )

time: 48.7 us -> 38.3 us (0.79)
  the two profiles are of different devices: /device:TPU:23 before, /device:TPU:205 now
where the time goes in v1:
time: 38.3 us; the launch traced here: 38.1 us
  waiting for transfers between devices  18.6 us (49%)
  Pallas kernels  11.4 us (30%)
  starting transfers between devices  8.07 us (21%)
    ppermute x2, waiting for transfers between devices, shifted(): return lax.ppermute(x, axis, pairs)  15.1 us
    pallas_call x1, Pallas kernels, second(): pl.pallas_call(functools.partial(second_kernel, at_end), out_shape=jax.Sh...  7.7 us
    ppermute x2, starting transfers between devices, shifted(): return lax.ppermute(x, axis, pairs)  5.4 us
    ppermute x3, waiting for transfers between devices, turned_down(): return lax.ppermute(x, axes if len(axes) > 1 else axes[0], pairs)  3.5 us
    ppermute x3, starting transfers between devices, turned_down(): return lax.ppermute(x, axes if len(axes) > 1 else axes[0], pairs)  2.67 us
    pallas_call x1, Pallas kernels, first(): pl.pallas_call(functools.partial(first_kernel, lasts), out_shape=tuple((j...  1.93 us
    pallas_call x1, Pallas kernels, strips(): pl.pallas_call(strips_kernel, grid=(1,), out_shape=(jax.ShapeDtypeStruct(...  1.78 us
  transfers between devices with their start and end apart: 5, of which 2 were waited for; matrix products, arithmetic and copies ran while one was open for 0% of the time, Pallas kernels for 10%

profile of v1, /device:TPU:205, one launch (start us, length us, event | category | flops | bytes accessed | tf_op | source)
XLA Modules:
  0.0 38.1 jit_solution(4815526398676127084)
XLA Ops:
  0.0 0.0 copy-start.3
  0.0 0.0 copy-start.5
  0.0 0.0 copy-start
  0.0 2.8 %collective-permute-start = (f32[256,512]{1,0:T(8,128)}, f32[256,512]{1,0:T(8,128)S(1)}, u32[]{:S(2)}, u32[]{:S(2)}) collective-permute-start(f32[256,512]{1,0:T(8,128)} %bitcast.1), channel_id=1, source_target_pairs={{16,0},{32,16},{48,32},{64,48},{80,64},{96,80},{112,96},{128,112},... | collective-permute-start | bytes 1572872 | tf_op jit(solution)/shard_map/ppermute | solution.py:374
  2.8 1.8 %strips.1 = (f32[2,32,512]{2,1,0:T(8,128)}, f32[2,64,128]{2,1,0:T(8,128)}, f32[2,8,128]{2,1,0:T(8,128)}) custom-call(f32[1,256,512]{2,1,0:T(8,128)} %col_ref.1, f32[1,256,512]{2,1,0:T(8,128)} %col_ref.1, f32[256,512]{1,0:T(8,128)} %following_ref.1, f32[256,512]{1,0:T(8,128)} %following_ref.1), custom_call_target="tpu_custom_call" | custom-call | tf_op jit(solution)/shard_map/strips/pallas_call | solution.py:259
  4.6 1.0 %collective-permute-start.1 = (f32[2,32,512]{2,1,0:T(8,128)}, f32[2,32,512]{2,1,0:T(8,128)S(1)}, u32[]{:S(2)}, u32[]{:S(2)}) collective-permute-start(f32[2,32,512]{2,1,0:T(8,128)} %get-tuple-element.12), channel_id=1, source_target_pairs={{0,14},{2,0},{4,2},{6,4},{8,6},{10,8},{12,10},{14,12},{1,15},{3,1}... | collective-permute-start | bytes 393224 | tf_op jit(solution)/shard_map/ppermute | solution.py:383
  5.5 0.9 %collective-permute-start.2 = (f32[2,64,128]{2,1,0:T(8,128)}, f32[2,64,128]{2,1,0:T(8,128)S(1)}, u32[]{:S(2)}, u32[]{:S(2)}) collective-permute-start(f32[2,64,128]{2,1,0:T(8,128)} %get-tuple-element.13), channel_id=1, source_target_pairs={{0,1},{1,0},{2,3},{3,2},{4,5},{5,4},{6,7},{7,6},{8,9},{9,8},{10,11... | collective-permute-start | bytes 196616 | tf_op jit(solution)/shard_map/ppermute | solution.py:383
  6.4 0.0 copy-start.1
  6.4 0.0 copy-start.2
  6.4 0.0 copy-start.4
  6.4 0.0 copy-start.6
  6.5 0.8 %collective-permute-start.3 = (f32[2,8,128]{2,1,0:T(8,128)}, f32[2,8,128]{2,1,0:T(8,128)S(1)}, u32[]{:S(2)}, u32[]{:S(2)}) collective-permute-start(f32[2,8,128]{2,1,0:T(8,128)} %get-tuple-element.14), channel_id=1, source_target_pairs={{0,15},{1,14},{2,1},{3,0},{4,3},{5,2},{6,5},{7,4},{8,7},{9,6},{10,... | collective-permute-start | bytes 24584 | tf_op jit(solution)/shard_map/ppermute | solution.py:383
  7.2 3.5 %collective-permute-done.3.corner_ref = f32[2,8,128]{2,1,0:T(8,128)S(1)} collective-permute-done((f32[2,8,128]{2,1,0:T(8,128)}, f32[2,8,128]{2,1,0:T(8,128)S(1)}, u32[]{:S(2)}, u32[]{:S(2)}) %collective-permute-start.3) | collective-permute-done | bytes 8224 | tf_op jit(solution)/shard_map/ppermute | solution.py:383
  10.7 0.0 collective-permute-done.2.col_ref
  10.7 0.0 collective-permute-done.1.row_ref
  10.7 0.0 copy-done.3
  10.8 0.0 copy-done.5
  10.8 0.0 copy-done
  10.8 1.9 %first.1 = (f32[8,8,64,128]{3,2,1,0:T(8,128)S(1)}, f32[3,8,640]{2,1,0:T(8,128)S(1)}, f32[200,128]{1,0:T(8,128)S(1)}, f32[200,128]{1,0:T(8,128)S(1)}) custom-call(f32[256,512]{1,0:T(8,128)S(1)} %bitcast.2, f32[2,32,512]{2,1,0:T(8,128)S(1)} %collective-permute-done.1.row_ref, f32[2,64,128]{2,1,0:T(8,128)S(1)} %collective-permute-done.2.col_ref, ...), custom_call_target="tpu_custom_call" | custom-call | flops 3000000000 | bytes 3145728 | tf_op jit(solution)/shard_map/first/pallas_call | solution.py:338
  12.7 2.6 %collective-permute-start.4 = (f32[200,128]{1,0:T(8,128)S(1)}, f32[200,128]{1,0:T(8,128)S(1)}, u32[]{:S(2)}, u32[]{:S(2)}) collective-permute-start(f32[200,128]{1,0:T(8,128)S(1)} %get-tuple-element.15), channel_id=1, source_target_pairs={{16,0},{32,16},{48,32},{64,48},{80,64},{96,80},{112,96},{128,112},... | collective-permute-start | bytes 307208 | tf_op jit(solution)/shard_map/ppermute | solution.py:374
  15.4 15.1 %collective-permute-done.4.rim_ref = f32[200,128]{1,0:T(8,128)S(1)} collective-permute-done((f32[200,128]{1,0:T(8,128)S(1)}, f32[200,128]{1,0:T(8,128)S(1)}, u32[]{:S(2)}, u32[]{:S(2)}) %collective-permute-start.4) | collective-permute-done | bytes 102432 | tf_op jit(solution)/shard_map/ppermute | solution.py:374
  30.4 0.0 collective-permute-done.tile_ref
  30.4 0.0 copy-done.1
  30.4 0.0 copy-done.2
  30.4 0.0 copy-done.4
  30.4 0.0 copy-done.6
  30.4 7.7 %second.1 = f32[1,8,64,1024]{3,2,1,0:T(8,128)} custom-call(f32[256,512]{1,0:T(8,128)S(1)} %collective-permute-done.tile_ref, f32[256,512]{1,0:T(8,128)S(1)} %copy-done.1, f32[200,128]{1,0:T(8,128)S(1)} %collective-permute-done.4.rim_ref, f32[200,128]{1,0:T(8,128)S(1)} %get-tuple-element.16.following_rim_ref, ...), custom_call_target="tpu_custom_call" | custom-call | flops 8000000000 | bytes 5242880 | tf_op jit(solution)/shard_map/second/pallas_call | solution.py:352
Async XLA Ops:
  0.0 10.8 %copy-start.3 = (bf16[384,256]{1,0:T(8,128)(2,1)S(1)}, bf16[384,256]{1,0:T(8,128)(2,1)}, u32[]{:S(2)}) copy-start(bf16[384,256]{1,0:T(8,128)(2,1)} %constant.11.clone.across_ref) | copy-start | bytes 589828
  0.0 10.8 %copy-start.5 = (bf16[64,192]{1,0:T(8,128)(2,1)S(1)}, bf16[64,192]{1,0:T(8,128)(2,1)}, u32[]{:S(2)}) copy-start(bf16[64,192]{1,0:T(8,128)(2,1)} %constant.10.clone.down_ref) | copy-start | bytes 73732
  0.0 10.8 %copy-start = (f32[1,256,512]{2,1,0:T(8,128)S(1)}, f32[1,256,512]{2,1,0:T(8,128)}, u32[]{:S(2)}) copy-start(f32[1,256,512]{2,1,0:T(8,128)} %col_ref.1) | copy-start | bytes 1572868
  0.0 30.4 %collective-permute-start = (f32[256,512]{1,0:T(8,128)}, f32[256,512]{1,0:T(8,128)S(1)}, u32[]{:S(2)}, u32[]{:S(2)}) collective-permute-start(f32[256,512]{1,0:T(8,128)} %bitcast.1), channel_id=1, source_target_pairs={{16,0},{32,16},{48,32},{64,48},{80,64},{96,80},{112,96},{128,112},... | collective-permute-start | bytes 1572872 | tf_op jit(solution)/shard_map/ppermute | solution.py:374
  4.6 6.2 %collective-permute-start.1 = (f32[2,32,512]{2,1,0:T(8,128)}, f32[2,32,512]{2,1,0:T(8,128)S(1)}, u32[]{:S(2)}, u32[]{:S(2)}) collective-permute-start(f32[2,32,512]{2,1,0:T(8,128)} %get-tuple-element.12), channel_id=1, source_target_pairs={{0,14},{2,0},{4,2},{6,4},{8,6},{10,8},{12,10},{14,12},{1,15},{3,1}... | collective-permute-start | bytes 393224 | tf_op jit(solution)/shard_map/ppermute | solution.py:383
  5.5 5.2 %collective-permute-start.2 = (f32[2,64,128]{2,1,0:T(8,128)}, f32[2,64,128]{2,1,0:T(8,128)S(1)}, u32[]{:S(2)}, u32[]{:S(2)}) collective-permute-start(f32[2,64,128]{2,1,0:T(8,128)} %get-tuple-element.13), channel_id=1, source_target_pairs={{0,1},{1,0},{2,3},{3,2},{4,5},{5,4},{6,7},{7,6},{8,9},{9,8},{10,11... | collective-permute-start | bytes 196616 | tf_op jit(solution)/shard_map/ppermute | solution.py:383
  6.4 24.0 %copy-start.1 = (f32[256,512]{1,0:T(8,128)S(1)}, f32[256,512]{1,0:T(8,128)}, u32[]{:S(2)}) copy-start(f32[256,512]{1,0:T(8,128)} %following_ref.1) | copy-start | bytes 1572868
  6.4 24.0 %copy-start.2 = (bf16[768,256]{1,0:T(8,128)(2,1)S(1)}, bf16[768,256]{1,0:T(8,128)(2,1)}, u32[]{:S(2)}) copy-start(bf16[768,256]{1,0:T(8,128)(2,1)} %constant.12.clone.fine_ref) | copy-start | bytes 1179652
  6.4 24.0 %copy-start.4 = (bf16[384,128]{1,0:T(8,128)(2,1)S(1)}, bf16[384,128]{1,0:T(8,128)(2,1)}, u32[]{:S(2)}) copy-start(bf16[384,128]{1,0:T(8,128)(2,1)} %constant.14.clone.sum_ref) | copy-start | bytes 294916
  6.4 24.0 %copy-start.6 = (bf16[64,192]{1,0:T(8,128)(2,1)S(1)}, bf16[64,192]{1,0:T(8,128)(2,1)}, u32[]{:S(2)}) copy-start(bf16[64,192]{1,0:T(8,128)(2,1)} %constant.13.clone.up_ref) | copy-start | bytes 73732
  6.5 4.3 %collective-permute-start.3 = (f32[2,8,128]{2,1,0:T(8,128)}, f32[2,8,128]{2,1,0:T(8,128)S(1)}, u32[]{:S(2)}, u32[]{:S(2)}) collective-permute-start(f32[2,8,128]{2,1,0:T(8,128)} %get-tuple-element.14), channel_id=1, source_target_pairs={{0,15},{1,14},{2,1},{3,0},{4,3},{5,2},{6,5},{7,4},{8,7},{9,6},{10,... | collective-permute-start | bytes 24584 | tf_op jit(solution)/shard_map/ppermute | solution.py:383
  12.7 17.7 %collective-permute-start.4 = (f32[200,128]{1,0:T(8,128)S(1)}, f32[200,128]{1,0:T(8,128)S(1)}, u32[]{:S(2)}, u32[]{:S(2)}) collective-permute-start(f32[200,128]{1,0:T(8,128)S(1)} %get-tuple-element.15), channel_id=1, source_target_pairs={{16,0},{32,16},{48,32},{64,48},{80,64},{96,80},{112,96},{128,112},... | collective-permute-start | bytes 307208 | tf_op jit(solution)/shard_map/ppermute | solution.py:374

commit v2 on v1

--- a/solution.py
+++ b/solution.py
@@ -17,6 +17,9 @@
 EPS = 1e-05
 F32 = jnp.float32
 BF16 = jnp.bfloat16
+ANY = pl.BlockSpec(memory_space=pl.ANY)
+VMEM = pl.BlockSpec(memory_space=pltpu.VMEM)
+STRIPS_VMEM = 60 << 20
 FIRST_VMEM = 8 << 20
 SECOND_VMEM = 16 << 20
 
@@ -90,13 +93,10 @@
 
 def column_block(pack, corner, b):
     blocks = 2 * LANES // STRIDE
-    if b < blocks:
-        return turned(pack[STRIDE * (b % 2) : STRIDE * (b % 2) + STRIDE, :], b // 2)
-    return jnp.concatenate([turned(corner, q) for q in range(LANES // STRIDE)], axis=0)
-
-
-def turned(x, quarter):
-    return pltpu.roll(x, LANES - STRIDE * quarter, 1) if quarter else x
+    if b == blocks:
+        return corner
+    block = pack[STRIDE * (b % 2) : STRIDE * (b % 2) + STRIDE]
+    return pltpu.roll(block, LANES - STRIDE * (b // 2), 1) if b // 2 else block
 
 
 def window_rows(tile, rims, i, down_count):
@@ -246,67 +246,81 @@
     return out
 
 
-def strips_kernel(row_ref, col_ref, next_row_ref, next_col_ref, out_row_ref, out_col_ref, out_corner_ref):
-    for n, (row, col) in enumerate(((row_ref, col_ref), (next_row_ref, next_col_ref))):
-        out_row_ref[n] = row[...].reshape(row.shape[-2:])
-        slab = col[...].reshape(col.shape[-2:])
-        out_col_ref[n] = packed_columns(slab)
-        out_corner_ref[n] = packed_columns(slab[:STRIDE])
-
-
-def strips(frames, following):
+def strips_kernel(row_ref, slab_ref, next_row_ref, next_slab_ref, out_row_ref, out_col_ref):
+    for n, (row, slab) in enumerate(((row_ref, slab_ref), (next_row_ref, next_slab_ref))):
+        out_col_ref[n] = packed_columns(slab[...])
+        for t in range(row.shape[1] // LANES):
+            out_row_ref[n, STRIDE * t : STRIDE * (t + 1), :] = row[:, LANES * t : LANES * (t + 1)]
+
+
+def strips(tile, following):
     height, breadth = following.shape
+    ends = [
+        pl.BlockSpec((STRIDE, breadth), lambda g: (0, 0)),
+        pl.BlockSpec((height, LANES), lambda g: (0, 0)),
+    ]
     return pl.pallas_call(
         strips_kernel,
         grid=(1,),
         out_shape=(
-            jax.ShapeDtypeStruct((2, STRIDE, breadth), F32),
+            jax.ShapeDtypeStruct((2, STRIDE * (breadth // LANES), LANES), F32),
             jax.ShapeDtypeStruct((2, height // 4, LANES), F32),
-            jax.ShapeDtypeStruct((2, STRIDE // 4, LANES), F32),
         ),
-        in_specs=[
-            pl.BlockSpec((1, STRIDE, breadth), lambda g: (0, 0, 0)),
-            pl.BlockSpec((1, height, LANES), lambda g: (0, 0, 0)),
-            pl.BlockSpec((STRIDE, breadth), lambda g: (0, 0)),
-            pl.BlockSpec((height, LANES), lambda g: (0, 0)),
-        ],
-        out_specs=(
-            pl.BlockSpec((2, STRIDE, breadth), lambda g: (0, 0, 0)),
-            pl.BlockSpec((2, height // 4, LANES), lambda g: (0, 0, 0)),
-            pl.BlockSpec((2, STRIDE // 4, LANES), lambda g: (0, 0, 0)),
-        ),
+        in_specs=ends * 2,
+        out_specs=(VMEM, VMEM),
+        compiler_params=pltpu.CompilerParams(vmem_limit_bytes=STRIPS_VMEM),
         name="strips",
-    )(frames, frames, following, following)
-
-
-def first_kernel(lasts, tile_ref, row_ref, col_ref, corner_ref, down_ref, across_ref, x_ref, stat_ref, send_ref, next_ref):
-    row_last, col_last = lasts()
-    for n, out in enumerate((send_ref, next_ref)):
-        row = jnp.where(row_last, 0.0, row_ref[n])
-        pack = jnp.where(col_last, 0.0, col_ref[n])
-        corner = jnp.where(jnp.logical_or(row_last, col_last), 0.0, corner_ref[n])
-        pieces = [row[:, LANES * t : LANES * (t + 1)] for t in range(row.shape[1] // LANES)]
-        out[...] = jnp.concatenate(pieces + [pack, corner], axis=0)
-        if n == 0:
-            rims = (row, pack, corner)
+    )(tile, tile, following, following)
+
+
+def join_kernel(upper_ref, lower_ref, out_ref):
+    height = upper_ref.shape[-2]
+    rows = out_ref.shape[-2] - height
+    if len(out_ref.shape) == 3:
+        out_ref[:, :height, :] = upper_ref[...]
+        out_ref[:, height:, :] = lower_ref[:, :rows, :]
+    else:
+        out_ref[:height, :] = upper_ref[0]
+        out_ref[height:, :] = lower_ref[0, :rows, :]
+
+
+def join(upper, lower, shape):
+    return pl.pallas_call(
+        join_kernel,
+        out_shape=jax.ShapeDtypeStruct(shape, F32),
+        in_specs=[VMEM, VMEM],
+        out_specs=VMEM,
+        compiler_params=pltpu.CompilerParams(vmem_limit_bytes=2 << 20),
+    )(upper, lower)
+
+
+def rims_of(rows, cols, row_last, col_last, tall):
+    tiles = jnp.where(row_last, 0.0, rows[:tall])
+    row = jnp.concatenate([tiles[STRIDE * t : STRIDE * (t + 1)] for t in range(tall // STRIDE)], axis=1)
+    corner = jnp.where(jnp.logical_or(row_last, col_last), 0.0, rows[tall:])
+    return row, jnp.where(col_last, 0.0, cols), corner
+
+
+def first_kernel(place, tile_ref, row_ref, col_ref, down_ref, across_ref, x_ref, stat_ref):
+    row_last, col_last, _ = place()
+    tall = STRIDE * (tile_ref.shape[1] // LANES)
+    rims = rims_of(row_ref[0], col_ref[0], row_last, col_last, tall)
     forward(tile_ref[...], rims, down_ref, across_ref, x_ref, stat_ref)
 
 
 def second_kernel(
-    at_end, tile_ref, following_ref, rim_ref, following_rim_ref, first_ref, first_stat,
+    place, tile_ref, following_ref, rim_ref, row_ref, col_ref, first_ref, first_stat,
     down_ref, across_ref, fine_ref, up_ref, sum_ref,
     out_ref,
     second_ref, second_stat, edge_ref, scale_ref, plane_ref, sems,
 ):
-    last = at_end()
+    row_last, col_last, last = place()
     tile = jnp.where(last, following_ref[...], tile_ref[...])
-    rim = jnp.where(last, following_rim_ref[...], rim_ref[...])
+    at = row_ref.shape[1]
+    rows = jnp.where(last, row_ref[1], rim_ref[0:at, :])
+    cols = jnp.where(last, col_ref[1], rim_ref[at:, :])
     tables = (down_ref, across_ref, fine_ref, up_ref, sum_ref)
-    count = tile.shape[1] // LANES
-    row = jnp.concatenate([rim[STRIDE * t : STRIDE * (t + 1)] for t in range(count)], axis=1)
-    at = STRIDE * count
-    rows = tile.shape[0] // 4
-    rims = (row, rim[at : at + rows], rim[at + rows : at + rows + STRIDE // 4])
+    rims = rims_of(rows, cols, row_last, col_last, at - STRIDE)
     forward(tile, rims, down_ref, across_ref, second_ref, second_stat)
     edge_rows(first_ref, second_ref, first_stat, second_stat, tables, edge_ref, scale_ref)
     copies = []
@@ -320,39 +334,32 @@
         copy.wait()
 
 
-ANY = pl.BlockSpec(memory_space=pl.ANY)
-VMEM = pl.BlockSpec(memory_space=pltpu.VMEM)
-
-
 def sizes(height, breadth):
     down_count = height // STRIDE
     tiles = 2 * breadth // LANES
-    spectrum = (down_count, tiles, W, LANES)
-    stat = (3, down_count, breadth + LANES)
-    rim = (STRIDE * (breadth // LANES) + height // 4 + STRIDE // 4, LANES)
-    return down_count, tiles, spectrum, stat, rim
-
-
-def first(tile, row, col, corner, lasts, tables):
-    _, _, spectrum, stat, rim = sizes(*tile.shape)
+    return down_count, tiles, (down_count, tiles, W, LANES), (3, down_count, breadth + LANES)
+
+
+def first(place, tile, rows, cols, tables):
+    _, _, spectrum, stat = sizes(*tile.shape)
     return pl.pallas_call(
-        functools.partial(first_kernel, lasts),
-        out_shape=tuple(jax.ShapeDtypeStruct(shape, F32) for shape in (spectrum, stat, rim, rim)),
-        in_specs=[VMEM] * 6,
-        out_specs=(VMEM,) * 4,
+        functools.partial(first_kernel, place),
+        out_shape=tuple(jax.ShapeDtypeStruct(shape, F32) for shape in (spectrum, stat)),
+        in_specs=[VMEM] * 5,
+        out_specs=(VMEM,) * 2,
         compiler_params=pltpu.CompilerParams(vmem_limit_bytes=FIRST_VMEM),
         cost_estimate=pl.CostEstimate(flops=3 * 10**9, bytes_accessed=3 << 20, transcendentals=0),
         name="first",
-    )(tile, row, col, corner, *tables[:2])
-
-
-def second(at_end, tile, following, rims, following_rims, spectrum, stat, tables):
+    )(tile, rows, cols, *tables[:2])
+
+
+def second(place, tile, following, rims, rows, cols, spectrum, stat, tables):
     height, breadth = tile.shape
-    down_count, tiles, shape, stat_shape, _ = sizes(height, breadth)
+    down_count, tiles, shape, stat_shape = sizes(height, breadth)
     return pl.pallas_call(
-        functools.partial(second_kernel, at_end),
+        functools.partial(second_kernel, place),
         out_shape=jax.ShapeDtypeStruct((1, down_count, W, 2 * breadth), F32),
-        in_specs=[VMEM] * 11,
+        in_specs=[VMEM] * 12,
         out_specs=ANY,
         scratch_shapes=[
             pltpu.VMEM(shape, F32),
@@ -365,46 +372,30 @@
         compiler_params=pltpu.CompilerParams(vmem_limit_bytes=SECOND_VMEM),
         cost_estimate=pl.CostEstimate(flops=8 * 10**9, bytes_accessed=5 << 20, transcendentals=0),
         name="second",
-    )(tile, following, rims, following_rims, spectrum, stat, *tables)
-
-
-def shifted(x, axis, by):
+    )(tile, following, rims, rows, cols, spectrum, stat, *tables)
+
+
+def turned_down(x, axis):
     devices = lax.axis_size(axis)
-    pairs = [(i, i + by) for i in range(devices) if 0 <= i + by < devices]
-    return lax.ppermute(x, axis, pairs)
-
-
-def turned_down(x, *axes):
-    counts = [lax.axis_size(axis) for axis in axes]
-    pairs = []
-    for source in np.ndindex(*counts):
-        target = tuple((s - 1) % n for s, n in zip(source, counts))
-        pairs.append((int(np.ravel_multi_index(source, counts)), int(np.ravel_multi_index(target, counts))))
-    return lax.ppermute(x, axes if len(axes) > 1 else axes[0], pairs)
-
-
-def lasts():
-    return (
-        lax.axis_index("row") == lax.axis_size("row") - 1,
-        lax.axis_index("col") == lax.axis_size("col") - 1,
-    )
-
-
-def at_end():
-    return lax.axis_index("tm") == lax.axis_size("tm") - 1
+    return lax.ppermute(x, axis, [(i, (i - 1) % devices) for i in range(devices)])
+
+
+def place():
+    return tuple(lax.axis_index(axis) == lax.axis_size(axis) - 1 for axis in ("row", "col", "tm"))
 
 
 def on_device(frames, following):
     tables = [jnp.asarray(t, BF16) for t in make_tables()]
     tile = frames[0]
-    arriving = shifted(tile, "tm", -1)
-    rows, cols, corners = strips(frames, following)
-    rows = turned_down(rows, "row")
+    rows, cols = strips(tile, following)
     cols = turned_down(cols, "col")
-    corners = turned_down(corners, "row", "col")
-    spectrum, stat, send, following_rims = first(tile, rows, cols, corners, lasts, tables)
-    rims = shifted(send, "tm", -1)
-    return second(at_end, arriving, following, rims, following_rims, spectrum, stat, tables)
+    arriving = turned_down(tile, "tm")
+    tall = rows.shape[1]
+    rows = turned_down(join(rows, cols, (2, tall + STRIDE, LANES)), "row")
+    whole = (tall + STRIDE + cols.shape[1], LANES)
+    rims = turned_down(join(rows, cols, whole), "tm")
+    spectrum, stat = first(place, tile, rows, cols, tables)
+    return second(place, arriving, following, rims, rows, cols, spectrum, stat, tables)
 
 
 def solution(mesh):

time: 38.3 us -> 42.8 us (1.12)
  the two profiles are of different devices: /device:TPU:205 before, /device:TPU:25 now
where the time goes in v2:
time: 42.8 us; the launch traced here: 42.7 us
  starting transfers between devices  22.7 us (53%)
  Pallas kernels  11.4 us (27%)
  waiting for transfers between devices  7.46 us (17%)
  local copies, waits for them, and re-layouts  0.94 us (2%)
    ppermute x4, starting transfers between devices, turned_down(): lax.ppermute(x, axis, [(i, (i - 1) % devices) for i in range(devices)])  22.7 us
    pallas_call x1, Pallas kernels, second(): pl.pallas_call(functools.partial(second_kernel, place), out_shape=jax.Sha...  7.72 us
    ppermute x4, waiting for transfers between devices, turned_down(): lax.ppermute(x, axis, [(i, (i - 1) % devices) for i in range(devices)])  7.46 us
    pallas_call x1, Pallas kernels, first(): pl.pallas_call(functools.partial(first_kernel, place), out_shape=tuple((j...  1.93 us
    pallas_call x1, Pallas kernels, strips(): pl.pallas_call(strips_kernel, grid=(1,), out_shape=(jax.ShapeDtypeStruct(...  1.77 us
    unnamed x16, local copies, waits for them, and re-layouts  0.94 us
  transfers between devices with their start and end apart: 4, of which 2 were waited for; matrix products, arithmetic and copies ran while one was open for 0% of the time, Pallas kernels for 9%

profile of v2, /device:TPU:25, one launch (start us, length us, event | category | flops | bytes accessed | tf_op | source)
XLA Modules:
  0.0 42.7 jit_solution(13512730773192819299)
XLA Ops:
  0.0 0.0 copy-start.4
  0.0 0.0 copy-start.6
  0.0 0.0 copy-start
  0.0 8.1 %collective-permute-start = (f32[256,512]{1,0:T(8,128)}, f32[256,512]{1,0:T(8,128)S(1)}, u32[]{:S(2)}, u32[]{:S(2)}) collective-permute-start(f32[256,512]{1,0:T(8,128)} %bitcast.1), channel_id=1, source_target_pairs={{0,240},{16,0},{32,16},{48,32},{64,48},{80,64},{96,80},{112,96},{1... | collective-permute-start | bytes 1572872 | tf_op jit(solution)/shard_map/ppermute | solution.py:380
  8.1 1.8 %strips.1 = (f32[2,128,128]{2,1,0:T(8,128)}, f32[2,64,128]{2,1,0:T(8,128)}) custom-call(f32[256,512]{1,0:T(8,128)} %bitcast.2, f32[256,512]{1,0:T(8,128)} %bitcast.3, f32[256,512]{1,0:T(8,128)} %following_ref.1, f32[256,512]{1,0:T(8,128)} %following_ref.1), custom_call_target="tpu_custom_call" | custom-call | tf_op jit(solution)/shard_map/strips/pallas_call | solution.py:262
  9.9 0.3 collective-permute-start.1
  10.2 3.3 %collective-permute-done.1.lower_ref.col_ref = f32[2,64,128]{2,1,0:T(8,128)S(1)} collective-permute-done((f32[2,64,128]{2,1,0:T(8,128)}, f32[2,64,128]{2,1,0:T(8,128)S(1)}, u32[]{:S(2)}, u32[]{:S(2)}) %collective-permute-start.1) | collective-permute-done | bytes 65568 | tf_op jit(solution)/shard_map/ppermute | solution.py:380
  13.5 0.0 copy-start.2
  13.5 0.9 %copy-done.2 = f32[2,128,128]{2,1,0:T(8,128)S(1)} copy-done((f32[2,128,128]{2,1,0:T(8,128)S(1)}, f32[2,128,128]{2,1,0:T(8,128)}, u32[]{:S(2)}) %copy-start.2) | copy-done | bytes 131096
  14.4 1.8 %collective-permute-start.2 = (f32[2,160,128]{2,1,0:T(8,128)S(1)}, f32[2,160,128]{2,1,0:T(8,128)S(1)}, u32[]{:S(2)}, u32[]{:S(2)}) collective-permute-start(f32[2,160,128]{2,1,0:T(8,128)S(1)} %shard_map.73), channel_id=1, source_target_pairs={{0,14},{2,0},{4,2},{6,4},{8,6},{10,8},{12,10},{14,12},{1,15},{3,1}... | collective-permute-start | bytes 491528 | tf_op jit(solution)/shard_map/ppermute | solution.py:380
  16.3 4.1 %collective-permute-done.2.upper_ref.row_ref = f32[2,160,128]{2,1,0:T(8,128)S(1)} collective-permute-done((f32[2,160,128]{2,1,0:T(8,128)S(1)}, f32[2,160,128]{2,1,0:T(8,128)S(1)}, u32[]{:S(2)}, u32[]{:S(2)}) %collective-permute-start.2) | collective-permute-done | bytes 163872 | tf_op jit(solution)/shard_map/ppermute | solution.py:380
  20.4 0.0 copy-start.1
  20.4 0.0 copy-start.3
  20.4 0.0 copy-start.5
  20.5 0.0 copy-start.7
  20.5 12.5 %collective-permute-start.3 = (f32[224,128]{1,0:T(8,128)S(1)}, f32[224,128]{1,0:T(8,128)S(1)}, u32[]{:S(2)}, u32[]{:S(2)}) collective-permute-start(f32[224,128]{1,0:T(8,128)S(1)} %shard_map.74), channel_id=1, source_target_pairs={{0,240},{16,0},{32,16},{48,32},{64,48},{80,64},{96,80},{112,96},{1... | collective-permute-start | bytes 344072 | tf_op jit(solution)/shard_map/ppermute | solution.py:380
  32.9 0.0 copy-done.4
  32.9 0.0 copy-done.6
  32.9 0.0 copy-done
  32.9 1.9 %first.1 = (f32[8,8,64,128]{3,2,1,0:T(8,128)S(1)}, f32[3,8,640]{2,1,0:T(8,128)S(1)}) custom-call(f32[256,512]{1,0:T(8,128)S(1)} %bitcast.4, f32[2,160,128]{2,1,0:T(8,128)S(1)} %collective-permute-done.2.upper_ref.row_ref, f32[2,64,128]{2,1,0:T(8,128)S(1)} %collective-permute-done.1.lower_ref.col_ref, bf16[64,192]{1,0:T(8,128)(2,1)S(1)} %copy-done.6, ...), custom_call_target="tpu_custom_call" | custom-call | flops 3000000000 | bytes 3145728 | tf_op jit(solution)/shard_map/first/pallas_call | solution.py:345
  34.9 0.0 collective-permute-done.3.rim_ref
  34.9 0.0 collective-permute-done.tile_ref
  34.9 0.0 copy-done.1
  34.9 0.0 copy-done.3
  34.9 0.0 copy-done.5
  34.9 0.0 copy-done.7
  34.9 7.7 %second.1 = f32[1,8,64,1024]{3,2,1,0:T(8,128)} custom-call(f32[256,512]{1,0:T(8,128)S(1)} %collective-permute-done.tile_ref, f32[256,512]{1,0:T(8,128)S(1)} %copy-done.1, f32[224,128]{1,0:T(8,128)S(1)} %collective-permute-done.3.rim_ref, f32[2,160,128]{2,1,0:T(8,128)S(1)} %collective-permute-done.2.upper_ref.row_ref, ...), custom_call_target="tpu_custom_call" | custom-call | flops 8000000000 | bytes 5242880 | tf_op jit(solution)/shard_map/second/pallas_call | solution.py:359
  (2 shorter events, 0.0 us)
Async XLA Ops:
  0.0 32.9 %copy-start.4 = (bf16[384,256]{1,0:T(8,128)(2,1)S(1)}, bf16[384,256]{1,0:T(8,128)(2,1)}, u32[]{:S(2)}) copy-start(bf16[384,256]{1,0:T(8,128)(2,1)} %constant.11.clone.across_ref) | copy-start | bytes 589828
  0.0 32.9 %copy-start.6 = (bf16[64,192]{1,0:T(8,128)(2,1)S(1)}, bf16[64,192]{1,0:T(8,128)(2,1)}, u32[]{:S(2)}) copy-start(bf16[64,192]{1,0:T(8,128)(2,1)} %constant.10.clone.down_ref) | copy-start | bytes 73732
  0.0 32.9 %copy-start = (f32[1,256,512]{2,1,0:T(8,128)S(1)}, f32[1,256,512]{2,1,0:T(8,128)}, u32[]{:S(2)}) copy-start(f32[1,256,512]{2,1,0:T(8,128)} %param.7) | copy-start | bytes 1572868
  0.0 34.9 %collective-permute-start = (f32[256,512]{1,0:T(8,128)}, f32[256,512]{1,0:T(8,128)S(1)}, u32[]{:S(2)}, u32[]{:S(2)}) collective-permute-start(f32[256,512]{1,0:T(8,128)} %bitcast.1), channel_id=1, source_target_pairs={{0,240},{16,0},{32,16},{48,32},{64,48},{80,64},{96,80},{112,96},{1... | collective-permute-start | bytes 1572872 | tf_op jit(solution)/shard_map/ppermute | solution.py:380
  9.9 3.6 %collective-permute-start.1 = (f32[2,64,128]{2,1,0:T(8,128)}, f32[2,64,128]{2,1,0:T(8,128)S(1)}, u32[]{:S(2)}, u32[]{:S(2)}) collective-permute-start(f32[2,64,128]{2,1,0:T(8,128)} %get-tuple-element.10), channel_id=1, source_target_pairs={{0,1},{1,0},{2,3},{3,2},{4,5},{5,4},{6,7},{7,6},{8,9},{9,8},{10,11... | collective-permute-start | bytes 196616 | tf_op jit(solution)/shard_map/ppermute | solution.py:380
  13.5 0.9 %copy-start.2 = (f32[2,128,128]{2,1,0:T(8,128)S(1)}, f32[2,128,128]{2,1,0:T(8,128)}, u32[]{:S(2)}) copy-start(f32[2,128,128]{2,1,0:T(8,128)} %get-tuple-element.9.upper_ref) | copy-start | bytes 393220
  14.4 6.0 %collective-permute-start.2 = (f32[2,160,128]{2,1,0:T(8,128)S(1)}, f32[2,160,128]{2,1,0:T(8,128)S(1)}, u32[]{:S(2)}, u32[]{:S(2)}) collective-permute-start(f32[2,160,128]{2,1,0:T(8,128)S(1)} %shard_map.73), channel_id=1, source_target_pairs={{0,14},{2,0},{4,2},{6,4},{8,6},{10,8},{12,10},{14,12},{1,15},{3,1}... | collective-permute-start | bytes 491528 | tf_op jit(solution)/shard_map/ppermute | solution.py:380
  20.4 14.5 %copy-start.1 = (f32[256,512]{1,0:T(8,128)S(1)}, f32[256,512]{1,0:T(8,128)}, u32[]{:S(2)}) copy-start(f32[256,512]{1,0:T(8,128)} %following_ref.1) | copy-start | bytes 1572868
  20.4 14.5 %copy-start.3 = (bf16[768,256]{1,0:T(8,128)(2,1)S(1)}, bf16[768,256]{1,0:T(8,128)(2,1)}, u32[]{:S(2)}) copy-start(bf16[768,256]{1,0:T(8,128)(2,1)} %constant.12.clone.fine_ref) | copy-start | bytes 1179652
  20.4 14.5 %copy-start.5 = (bf16[384,128]{1,0:T(8,128)(2,1)S(1)}, bf16[384,128]{1,0:T(8,128)(2,1)}, u32[]{:S(2)}) copy-start(bf16[384,128]{1,0:T(8,128)(2,1)} %constant.14.clone.sum_ref) | copy-start | bytes 294916
  20.5 14.5 %copy-start.7 = (bf16[64,192]{1,0:T(8,128)(2,1)S(1)}, bf16[64,192]{1,0:T(8,128)(2,1)}, u32[]{:S(2)}) copy-start(bf16[64,192]{1,0:T(8,128)(2,1)} %constant.13.clone.up_ref) | copy-start | bytes 73732
  20.5 14.4 %collective-permute-start.3 = (f32[224,128]{1,0:T(8,128)S(1)}, f32[224,128]{1,0:T(8,128)S(1)}, u32[]{:S(2)}, u32[]{:S(2)}) collective-permute-start(f32[224,128]{1,0:T(8,128)S(1)} %shard_map.74), channel_id=1, source_target_pairs={{0,240},{16,0},{32,16},{48,32},{64,48},{80,64},{96,80},{112,96},{1... | collective-permute-start | bytes 344072 | tf_op jit(solution)/shard_map/ppermute | solution.py:380
